TPU v7x, 128 devices: a whole 4x4x4 slice. The times are simulated.
128 devices in a mesh: mem: 32 (over x, z, core), head: 4 (over y).
Axes of the slice: x: 4, y: 4, z: 4, core: 2. Of those that a mesh axis runs over, the one named last changes fastest.
Arguments:
- queries: bfloat16 [512, 32, 128], P('mem', 'head'), may hold values from -170 to 170
- cache_blocks: bfloat16 [1024, 2, 8, 64, 128], P('mem', None, 'head'), may hold values from -9 to 9
- selected: int32 [512, 32], P('mem'), may hold values from 0 to 1023, as said below
- counts: int32 [16, 1024], P(None, 'mem'), may hold values from 0 to 8
- output_weight: bfloat16 [4096, 4096], P('head'), may hold values from -0.09375 to 0.09375
Outputs:
- layer_out: bfloat16 [512, 4096], P('mem', 'head')
- block_heat: float32 [1024], P('mem')
Inputs may be any that keep to these rules, and one draw needn't show every extreme that they name: `selected`: each request names 32 different blocks; at most 2 of a request's blocks b share the same b // 32.
All inputs are finite; a program needn't handle non-finite values.
Results may differ from a plain program's by a relative error of at most 0.012.
Values may be sent and summed in bfloat16 or wider, within the bound.
A program may use at most 128 MiB of HBM per device.

v0:
```python
import math

import jax
import jax.numpy as jnp
from jax import lax
from jax.sharding import PartitionSpec as P

NEGATIVE = -1e30


def cut_along(array, dim, length):
    lengths = array.shape
    pieces = array.reshape(*lengths[:dim], length, lengths[dim] // length, *lengths[dim + 1 :])
    return jnp.moveaxis(pieces, dim, 0)


def sent_and_summed(array, axis, dim):
    length = lax.axis_size(axis)
    pieces = lax.all_to_all(cut_along(array, dim, length), axis, 0, 0, tiled=True)
    return jnp.sum(pieces, axis=0)


def resident_partial(query_rows, block_ids, key_rows, value_rows):
    scores = jnp.einsum(
        "shgd,bhtd->shgbt", query_rows, key_rows, preferred_element_type=jnp.float32
    ) * query_rows.shape[-1] ** (-0.5)
    mine = (block_ids[:, None] == jnp.arange(key_rows.shape[0], dtype=jnp.int32)[None, :])[
        :, None, None, :, None
    ]
    masked = jnp.where(mine, scores, NEGATIVE)
    peak_score = jnp.max(masked, axis=(-2, -1))
    expo_terms = jnp.exp(masked - peak_score[..., None, None])
    totals = jnp.sum(expo_terms, axis=(-2, -1))
    weights = expo_terms.astype(jnp.bfloat16)
    outputs = jnp.einsum(
        "shgbt,bhtd->shgd", weights, value_rows, preferred_element_type=jnp.float32
    )
    return (peak_score, totals, outputs)


def attend_slots(cache_blocks, query_slots, block_slots):
    slots = query_slots.shape[0]
    heads_kv = cache_blocks.shape[2]
    head_dim = cache_blocks.shape[-1]
    group_size = math.gcd(slots, 128)
    grouped_queries = query_slots.reshape(slots // group_size, group_size, heads_kv, -1, head_dim)
    grouped_blocks = block_slots.reshape(slots // group_size, group_size)
    key_rows = cache_blocks[:, 0]
    value_rows = cache_blocks[:, 1]

    def one_group(inputs):
        queries_here, blocks_here = inputs
        return resident_partial(queries_here, blocks_here, key_rows, value_rows)

    peak_score, totals, outputs = lax.map(one_group, (grouped_queries, grouped_blocks))
    return (
        peak_score.reshape(slots, heads_kv, -1),
        totals.reshape(slots, heads_kv, -1),
        outputs.reshape(slots, heads_kv, -1, head_dim),
    )


def per_device(queries, cache_blocks, selected, counts, output_weight):
    devices_mem = lax.axis_size("mem")
    local_requests, local_heads, head_dim = queries.shape
    heads_kv = cache_blocks.shape[2]
    group_q = local_heads // heads_kv
    blocks_each = cache_blocks.shape[0]
    picks = selected.shape[1]
    most_each = max(2, 2 * picks // devices_mem)
    capacity = local_requests * most_each
    pair_count = local_requests * picks
    row_width = local_heads * head_dim
    flat_ids = selected.reshape(pair_count)
    target = flat_ids // blocks_each
    local_block = flat_ids % blocks_each
    owner_request = jnp.arange(pair_count, dtype=jnp.int32) // picks
    onehot = (target[:, None] == jnp.arange(devices_mem, dtype=jnp.int32)[None, :]).astype(
        jnp.int32
    )
    slot_index = jnp.sum((jnp.cumsum(onehot, axis=0) - onehot) * onehot, axis=1)
    position = target * capacity + slot_index
    access_hits = jnp.zeros((devices_mem * blocks_each,), jnp.float32).at[flat_ids].add(1.0)
    access_hits = sent_and_summed(access_hits, "mem", 0)
    decays = 0.5 ** jnp.arange(counts.shape[0], dtype=jnp.float32)
    block_heat = jnp.sum(decays[:, None] * counts.astype(jnp.float32), axis=0) + access_hits
    query_pairs = queries.reshape(local_requests, row_width)[owner_request]
    send_queries = (
        jnp.zeros((devices_mem * capacity, row_width), jnp.bfloat16).at[position].set(query_pairs)
    )
    labels = jnp.stack([local_block, owner_request], axis=1).astype(jnp.bfloat16)
    send_labels = jnp.full((devices_mem * capacity, 2), -1.0, jnp.bfloat16).at[position].set(labels)
    recv_queries, recv_labels = (
        lax.all_to_all(
            send_queries.reshape(devices_mem, capacity, row_width),
            "mem",
            split_axis=0,
            concat_axis=0,
            tiled=True,
        ),
        lax.all_to_all(
            send_labels.reshape(devices_mem, capacity, 2),
            "mem",
            split_axis=0,
            concat_axis=0,
            tiled=True,
        ),
    )
    query_slots = recv_queries.reshape(devices_mem * capacity, row_width)
    recv_labels = recv_labels.reshape(devices_mem * capacity, 2).astype(jnp.int32)
    block_slots = jnp.maximum(recv_labels[:, 0], 0)
    request_slots = recv_labels[:, 1]
    peak_score, totals, outputs = attend_slots(cache_blocks, query_slots, block_slots)
    member = (
        request_slots.reshape(devices_mem, capacity)[:, :, None]
        == jnp.arange(local_requests, dtype=jnp.int32)[None, None, :]
    )[..., None, None]
    slot_peak = peak_score.reshape(devices_mem, capacity, 1, heads_kv, group_q)
    source_peak = jnp.max(jnp.where(member, slot_peak, NEGATIVE), axis=1)
    factor = jnp.exp(jnp.where(member, slot_peak - source_peak[:, None], NEGATIVE))
    source_totals = jnp.sum(
        factor * totals.reshape(devices_mem, capacity, 1, heads_kv, group_q), axis=1
    )
    source_outputs = jnp.einsum(
        "scrhg,schgd->srhgd",
        factor,
        outputs.reshape(devices_mem, capacity, heads_kv, group_q, head_dim),
        precision=lax.Precision.HIGHEST,
    )
    back_peak, back_totals, back_outputs = (
        lax.all_to_all(source_peak, "mem", split_axis=0, concat_axis=0, tiled=True),
        lax.all_to_all(source_totals, "mem", split_axis=0, concat_axis=0, tiled=True),
        lax.all_to_all(source_outputs, "mem", split_axis=0, concat_axis=0, tiled=True),
    )
    highest = jnp.max(back_peak, axis=0)
    scale_back = jnp.exp(back_peak - highest[None])
    denominator = jnp.sum(scale_back * back_totals, axis=0)
    numerator = jnp.sum(scale_back[..., None] * back_outputs, axis=0)
    attended = (
        (numerator / denominator[..., None]).reshape(local_requests, row_width).astype(jnp.bfloat16)
    )
    partial_out = jnp.dot(attended, output_weight, preferred_element_type=jnp.float32)
    layer_out = lax.psum_scatter(
        partial_out.astype(jnp.bfloat16), "head", scatter_dimension=1, tiled=True
    )
    return (layer_out, block_heat)


def solution(mesh):
    return jax.shard_map(
        per_device,
        mesh=mesh,
        in_specs=(
            P("mem", "head", None),
            P("mem", None, "head", None, None),
            P("mem", None),
            P(None, "mem"),
            P("head", None),
        ),
        out_specs=(P("mem", "head"), P("mem")),
        check_vma=False,
    )
```

profile of v0, /device:TPU:1, one launch (start us, length us, event | category | flops | bytes accessed | tf_op | source)
XLA Modules:
  0.0 221.5 jit_solution(8425089687027608353)
XLA Ops:
  11.3 1.8 scatter_custom_fusion
  14.0 9.4 %all-to-all-start = ((bf16[32,32,2]{1,2,0:T(2,128)(2,1)}), bf16[32,32,2]{1,2,0:T(2,128)(2,1)S(1)}, u32[]{:S(2)}, u32[]{:S(2)}) async-start(bf16[32,32,2]{1,2,0:T(2,128)(2,1)} %copy.95), calls=%async_computation | async-start | bytes 32768 | tf_op jit(solution)/shard_map/all_to_all | solution.py:101
  24.2 7.7 %scatter_custom_fusion.1 = bf16[1024,1024]{1,0:T(8,128)(2,1)} fusion(s32[512]{0:T(512)S(1)} %bitcast.144, bf16[16,1024]{1,0:T(8,128)(2,1)S(1)} %bitcast.138, s32[1024]{0:T(1024)S(1)} %pad_clamp_fusion, bf16[]{:T(256)} %constant.84.clone.1), kind=kCustom, calls=%fused_computation.34 | custom fusion | bytes 2097154 | tf_op jit(solution)/shard_map/scatter | solution.py:89
  32.0 7.4 %all-to-all-start.1 = ((bf16[32,32,1024]{2,1,0:T(8,128)(2,1)}), bf16[32,32,1024]{2,1,0:T(8,128)(2,1)S(1)}, u32[]{:S(2)}, u32[]{:S(2)}) async-start(bf16[32,32,1024]{2,1,0:T(8,128)(2,1)} %bitcast.21), calls=%async_computation.1 | async-start | bytes 4194304 | tf_op jit(solution)/shard_map/all_to_all | solution.py:94
  39.4 1.7 fusion.45
  42.6 25.2 %all-to-all-done.1 = bf16[32,32,1024]{2,1,0:T(8,128)(2,1)S(1)} async-done(((bf16[32,32,1024]{2,1,0:T(8,128)(2,1)}), bf16[32,32,1024]{2,1,0:T(8,128)(2,1)S(1)}, u32[]{:S(2)}, u32[]{:S(2)}) %all-to-all-start.1) | async-done | bytes 2097184 | tf_op jit(solution)/shard_map/all_to_all | solution.py:94
  67.7 2.7 %reshape_reshape.8 = bf16[8,128,2,4,128]{4,3,2,1,0:T(4,128)(2,1)} reshape(bf16[32,32,1024]{2,1,0:T(8,128)(2,1)S(1)} %all-to-all-done.1) | data formatting | bytes 4194304 | tf_op jit(solution)/shard_map/reshape;reshape | solution.py:46
  70.4 60.0 %while.14 = (s32[]{:T(128)}, f32[8,128,2,4]{1,0,3,2:T(8,128)S(1)}, f32[8,128,2,4]{1,0,3,2:T(8,128)S(1)}, f32[8,128,2,4,128]{4,1,0,3,2:T(8,128)}, s32[8,128]{1,0:...) while((s32[]{:T(128)}, f32[8,128,2,4]{1,0,3,2:T(8,128)S(1)}, ...), condition=%wide.region_8.9_spmd, body=%wide.region_5.8_spmd.sunk | while | flops 1096812544 | bytes 32819344 | solution.py:55
  72.8 3.4 %fusion.57 = f32[8,128,2,4,128]{4,1,0,3,2:T(8,128)} fusion(f32[8,128,2,4,128]{4,1,0,3,2:T(8,128)} %get-tuple-element.201, s32[]{:T(128)} %get-tuple-element.198, f32[2,128,4,32,64]{1,4,3,2,0:T(8,128)S(1)} %get-tuple-element.187, f32[128,2,4]{0,2,1:T(4,128)S(1)} %get-tuple-element.186, pred[128,32]{0,1:T(8,128)(4,1)S(1)} %iota_compare_fusion.5, ...), kind=kOutput, calls=%fused_computation.13.clone.1 | convolution fusion | flops 545259520 | bytes 9970176 | tf_op jit(solution)/shard_map/while/body/eval_jaxpr/shgbt,bhtd->shgd/dot_general | solution.py:35
  80.3 3.3 %fusion.57 = f32[8,128,2,4,128]{4,1,0,3,2:T(8,128)} fusion(f32[8,128,2,4,128]{4,1,0,3,2:T(8,128)} %get-tuple-element.201, s32[]{:T(128)} %get-tuple-element.198, f32[2,128,4,32,64]{1,4,3,2,0:T(8,128)S(1)} %get-tuple-element.187, f32[128,2,4]{0,2,1:T(4,128)S(1)} %get-tuple-element.186, pred[128,32]{0,1:T(8,128)(4,1)S(1)} %iota_compare_fusion.5, ...), kind=kOutput, calls=%fused_computation.13.clone.1 | convolution fusion | flops 545259520 | bytes 9970176 | tf_op jit(solution)/shard_map/while/body/eval_jaxpr/shgbt,bhtd->shgd/dot_general | solution.py:35
  87.8 3.3 %fusion.57 = f32[8,128,2,4,128]{4,1,0,3,2:T(8,128)} fusion(f32[8,128,2,4,128]{4,1,0,3,2:T(8,128)} %get-tuple-element.201, s32[]{:T(128)} %get-tuple-element.198, f32[2,128,4,32,64]{1,4,3,2,0:T(8,128)S(1)} %get-tuple-element.187, f32[128,2,4]{0,2,1:T(4,128)S(1)} %get-tuple-element.186, pred[128,32]{0,1:T(8,128)(4,1)S(1)} %iota_compare_fusion.5, ...), kind=kOutput, calls=%fused_computation.13.clone.1 | convolution fusion | flops 545259520 | bytes 9970176 | tf_op jit(solution)/shard_map/while/body/eval_jaxpr/shgbt,bhtd->shgd/dot_general | solution.py:35
  91.1 1.7 fusion.56
  95.3 3.3 %fusion.57 = f32[8,128,2,4,128]{4,1,0,3,2:T(8,128)} fusion(f32[8,128,2,4,128]{4,1,0,3,2:T(8,128)} %get-tuple-element.201, s32[]{:T(128)} %get-tuple-element.198, f32[2,128,4,32,64]{1,4,3,2,0:T(8,128)S(1)} %get-tuple-element.187, f32[128,2,4]{0,2,1:T(4,128)S(1)} %get-tuple-element.186, pred[128,32]{0,1:T(8,128)(4,1)S(1)} %iota_compare_fusion.5, ...), kind=kOutput, calls=%fused_computation.13.clone.1 | convolution fusion | flops 545259520 | bytes 9970176 | tf_op jit(solution)/shard_map/while/body/eval_jaxpr/shgbt,bhtd->shgd/dot_general | solution.py:35
  98.6 1.7 fusion.56
  102.8 3.3 %fusion.57 = f32[8,128,2,4,128]{4,1,0,3,2:T(8,128)} fusion(f32[8,128,2,4,128]{4,1,0,3,2:T(8,128)} %get-tuple-element.201, s32[]{:T(128)} %get-tuple-element.198, f32[2,128,4,32,64]{1,4,3,2,0:T(8,128)S(1)} %get-tuple-element.187, f32[128,2,4]{0,2,1:T(4,128)S(1)} %get-tuple-element.186, pred[128,32]{0,1:T(8,128)(4,1)S(1)} %iota_compare_fusion.5, ...), kind=kOutput, calls=%fused_computation.13.clone.1 | convolution fusion | flops 545259520 | bytes 9970176 | tf_op jit(solution)/shard_map/while/body/eval_jaxpr/shgbt,bhtd->shgd/dot_general | solution.py:35
  106.1 1.7 fusion.56
  110.3 3.4 %fusion.57 = f32[8,128,2,4,128]{4,1,0,3,2:T(8,128)} fusion(f32[8,128,2,4,128]{4,1,0,3,2:T(8,128)} %get-tuple-element.201, s32[]{:T(128)} %get-tuple-element.198, f32[2,128,4,32,64]{1,4,3,2,0:T(8,128)S(1)} %get-tuple-element.187, f32[128,2,4]{0,2,1:T(4,128)S(1)} %get-tuple-element.186, pred[128,32]{0,1:T(8,128)(4,1)S(1)} %iota_compare_fusion.5, ...), kind=kOutput, calls=%fused_computation.13.clone.1 | convolution fusion | flops 545259520 | bytes 9970176 | tf_op jit(solution)/shard_map/while/body/eval_jaxpr/shgbt,bhtd->shgd/dot_general | solution.py:35
  113.7 1.7 fusion.56
  117.8 3.3 %fusion.57 = f32[8,128,2,4,128]{4,1,0,3,2:T(8,128)} fusion(f32[8,128,2,4,128]{4,1,0,3,2:T(8,128)} %get-tuple-element.201, s32[]{:T(128)} %get-tuple-element.198, f32[2,128,4,32,64]{1,4,3,2,0:T(8,128)S(1)} %get-tuple-element.187, f32[128,2,4]{0,2,1:T(4,128)S(1)} %get-tuple-element.186, pred[128,32]{0,1:T(8,128)(4,1)S(1)} %iota_compare_fusion.5, ...), kind=kOutput, calls=%fused_computation.13.clone.1 | convolution fusion | flops 545259520 | bytes 9970176 | tf_op jit(solution)/shard_map/while/body/eval_jaxpr/shgbt,bhtd->shgd/dot_general | solution.py:35
  121.2 1.7 fusion.56
  125.3 3.4 %fusion.57 = f32[8,128,2,4,128]{4,1,0,3,2:T(8,128)} fusion(f32[8,128,2,4,128]{4,1,0,3,2:T(8,128)} %get-tuple-element.201, s32[]{:T(128)} %get-tuple-element.198, f32[2,128,4,32,64]{1,4,3,2,0:T(8,128)S(1)} %get-tuple-element.187, f32[128,2,4]{0,2,1:T(4,128)S(1)} %get-tuple-element.186, pred[128,32]{0,1:T(8,128)(4,1)S(1)} %iota_compare_fusion.5, ...), kind=kOutput, calls=%fused_computation.13.clone.1 | convolution fusion | flops 545259520 | bytes 9970176 | tf_op jit(solution)/shard_map/while/body/eval_jaxpr/shgbt,bhtd->shgd/dot_general | solution.py:35
  128.7 1.7 fusion.56
  133.7 4.2 %all-to-all-start.4 = ((f32[32,1,128]{2,1,0:T(1,128)}), f32[32,1,128]{2,1,0:T(1,128)S(1)}, u32[]{:S(2)}, u32[]{:S(2)}) async-start(f32[32,1,128]{2,1,0:T(1,128)} %reshape.355), calls=%async_computation.4 | async-start | bytes 32768 | tf_op jit(solution)/shard_map/all_to_all | solution.py:132
  138.7 6.3 %all-to-all-done.4 = f32[32,1,128]{2,1,0:T(1,128)S(1)} async-done(((f32[32,1,128]{2,1,0:T(1,128)}), f32[32,1,128]{2,1,0:T(1,128)S(1)}, u32[]{:S(2)}, u32[]{:S(2)}) %all-to-all-start.4) | async-done | bytes 16416 | tf_op jit(solution)/shard_map/all_to_all | solution.py:132
  145.0 4.1 %all-to-all-start.2 = ((f32[32,1,128]{2,1,0:T(1,128)}), f32[32,1,128]{2,1,0:T(1,128)S(1)}, u32[]{:S(2)}, u32[]{:S(2)}) async-start(f32[32,1,128]{2,1,0:T(1,128)} %reshape.353), calls=%async_computation.2 | async-start | bytes 32768 | tf_op jit(solution)/shard_map/all_to_all | solution.py:131
  149.2 6.9 %fusion.20 = f32[32,16,2,4,128]{4,1,3,2,0:T(8,128)} fusion(f32[32,32,2,4,128]{4,1,0,3,2:T(8,128)} %bitcast.130, f32[32,16,2,4]{1,3,2,0:T(4,128)S(1)} %select_reduce_fusion, f32[32,32,2,4]{1,3,2,0:T(4,128)S(1)} %copy.101, pred[32,32,16]{1,2,0:T(8,128)(4,1)S(1)} %iota_compare_fusion.1), kind=kOutput, calls=%fused_computation.31 | convolution fusion | flops 201588736 | bytes 6356992 | tf_op jit(solution)/shard_map/scrhg,schgd->srhgd/dot_general | solution.py:124
  156.2 7.4 %all-to-all-start.3 = ((f32[32,16,2,4,128]{4,1,3,2,0:T(8,128)}), f32[32,16,2,4,128]{4,1,3,2,0:T(8,128)S(1)}, u32[]{:S(2)}, u32[]{:S(2)}) async-start(f32[32,16,2,4,128]{4,1,3,2,0:T(8,128)} %fusion.20), calls=%async_computation.3 | async-start | bytes 4194304 | tf_op jit(solution)/shard_map/all_to_all | solution.py:133
  166.1 25.8 %all-to-all-done.3 = f32[32,16,2,4,128]{4,1,3,2,0:T(8,128)S(1)} async-done(((f32[32,16,2,4,128]{4,1,3,2,0:T(8,128)}), f32[32,16,2,4,128]{4,1,3,2,0:T(8,128)S(1)}, u32[]{:S(2)}, u32[]{:S(2)}) %all-to-all-start.3) | async-done | bytes 2097184 | tf_op jit(solution)/shard_map/all_to_all | solution.py:133
  192.7 5.2 %convolution_convert_fusion = bf16[16,4096]{1,0:T(8,128)(2,1)} fusion(bf16[16,1024]{1,0:T(8,128)(2,1)S(1)} %convert_element_type.34, bf16[1024,4096]{1,0:T(8,128)(2,1)} %param.11), kind=kOutput, calls=%fused_computation.24 | convolution fusion | flops 134283264 | bytes 8552448 | tf_op jit(solution)/shard_map/dot_general | solution.py:142
  198.0 4.1 %scatter_custom_fusion.2 = f32[1024]{0:T(1024)S(1)} fusion(s32[512]{0:T(512)S(1)} %bitcast.142, f32[512]{0:T(512)S(1)} %broadcast.295, f32[]{:T(128)} %constant.83.clone.1), kind=kCustom, calls=%fused_computation.86 | custom fusion | flops 512 | bytes 4100 | tf_op jit(solution)/shard_map/scatter-add | solution.py:83
  202.8 4.2 %all-to-all-start.5 = ((f32[32,1,32]{2,1,0:T(1,128)}), f32[32,1,32]{2,1,0:T(1,128)S(1)}, u32[]{:S(2)}, u32[]{:S(2)}) async-start(f32[32,1,32]{2,1,0:T(1,128)} %all_to_all.26), calls=%async_computation.6 | async-start | bytes 32768 | tf_op jit(solution)/shard_map/all_to_all | solution.py:19
  207.1 7.0 %all-to-all-done.5 = f32[32,1,32]{2,1,0:T(1,128)S(1)} async-done(((f32[32,1,32]{2,1,0:T(1,128)}), f32[32,1,32]{2,1,0:T(1,128)S(1)}, u32[]{:S(2)}, u32[]{:S(2)}) %all-to-all-start.5) | async-done | bytes 4128 | tf_op jit(solution)/shard_map/all_to_all | solution.py:19
  (125 shorter events, 38.6 us)
Async XLA Ops:
  14.0 18.0 %all-to-all-start = ((bf16[32,32,2]{1,2,0:T(2,128)(2,1)}), bf16[32,32,2]{1,2,0:T(2,128)(2,1)S(1)}, u32[]{:S(2)}, u32[]{:S(2)}) async-start(bf16[32,32,2]{1,2,0:T(2,128)(2,1)} %copy.95), calls=%async_computation | async-start | bytes 32768 | tf_op jit(solution)/shard_map/all_to_all | solution.py:101
  32.0 35.7 %all-to-all-start.1 = ((bf16[32,32,1024]{2,1,0:T(8,128)(2,1)}), bf16[32,32,1024]{2,1,0:T(8,128)(2,1)S(1)}, u32[]{:S(2)}, u32[]{:S(2)}) async-start(bf16[32,32,1024]{2,1,0:T(8,128)(2,1)} %bitcast.21), calls=%async_computation.1 | async-start | bytes 4194304 | tf_op jit(solution)/shard_map/all_to_all | solution.py:94
  71.5 1.3 copy-start
  79.0 1.3 copy-start
  86.5 1.3 copy-start
  94.0 1.3 copy-start
  101.5 1.3 copy-start
  109.0 1.3 copy-start
  116.5 1.3 copy-start
  124.0 1.3 copy-start
  133.7 11.3 %all-to-all-start.4 = ((f32[32,1,128]{2,1,0:T(1,128)}), f32[32,1,128]{2,1,0:T(1,128)S(1)}, u32[]{:S(2)}, u32[]{:S(2)}) async-start(f32[32,1,128]{2,1,0:T(1,128)} %reshape.355), calls=%async_computation.4 | async-start | bytes 32768 | tf_op jit(solution)/shard_map/all_to_all | solution.py:132
  145.0 11.2 %all-to-all-start.2 = ((f32[32,1,128]{2,1,0:T(1,128)}), f32[32,1,128]{2,1,0:T(1,128)S(1)}, u32[]{:S(2)}, u32[]{:S(2)}) async-start(f32[32,1,128]{2,1,0:T(1,128)} %reshape.353), calls=%async_computation.2 | async-start | bytes 32768 | tf_op jit(solution)/shard_map/all_to_all | solution.py:131
  156.2 35.7 %all-to-all-start.3 = ((f32[32,16,2,4,128]{4,1,3,2,0:T(8,128)}), f32[32,16,2,4,128]{4,1,3,2,0:T(8,128)S(1)}, u32[]{:S(2)}, u32[]{:S(2)}) async-start(f32[32,16,2,4,128]{4,1,3,2,0:T(8,128)} %fusion.20), calls=%async_computation.3 | async-start | bytes 4194304 | tf_op jit(solution)/shard_map/all_to_all | solution.py:133
  163.5 51.1 %reduce-scatter.2.cloned.1.call-start = ((), (), s32[]{:S(2)}) async-start(), calls=%async_computation.7 | async-start | bytes 163840 | tf_op jit(solution)/shard_map/reduce_scatter | solution.py:143
  192.7 14.3 %copy-start.1 = (s32[16,32]{1,0:T(8,128)S(1)}, s32[16,32]{1,0:T(8,128)}, u32[]{:S(2)}) copy-start(s32[16,32]{1,0:T(8,128)} %param.10) | copy-start | bytes 6148
  202.8 11.3 %all-to-all-start.5 = ((f32[32,1,32]{2,1,0:T(1,128)}), f32[32,1,32]{2,1,0:T(1,128)S(1)}, u32[]{:S(2)}, u32[]{:S(2)}) async-start(f32[32,1,32]{2,1,0:T(1,128)} %all_to_all.26), calls=%async_computation.6 | async-start | bytes 32768 | tf_op jit(solution)/shard_map/all_to_all | solution.py:19
Sparse Core Ops, SparseCore 0:
  198.1 16.1 reduce-scatter.1
where the time goes:
time: 224 us; the launch traced here: 221 us
  waiting for transfers between devices  64.3 us (29%)
  matrix products  49 us (22%)
  starting transfers between devices  37 us (17%)
  local copies, waits for them, and re-layouts  32.1 us (14%)
  other arithmetic  24.1 us (11%)
  between operations  14.3 us (6%)
    dot_general x8, matrix products, resident_partial(): jnp.einsum('shgbt,bhtd->shgd', weights, value_rows, preferred_element_typ...  26.8 us
    all_to_all x1, waiting for transfers between devices, per_device(): lax.all_to_all(source_outputs, 'mem', split_axis=0, concat_axis=0, tiled=...  25.8 us
    all_to_all x1, waiting for transfers between devices, per_device(): lax.all_to_all(send_queries.reshape(devices_mem, capacity, row_width), 'm...  25.2 us
    reduce_sum x8, other arithmetic, resident_partial(): totals = jnp.sum(expo_terms, axis=(-2, -1))  13.5 us
    dot_general x8, matrix products, resident_partial(): jnp.einsum('shgd,bhtd->shgbt', query_rows, key_rows, preferred_element_ty...  10.1 us
    all_to_all x1, starting transfers between devices, per_device(): lax.all_to_all(send_labels.reshape(devices_mem, capacity, 2), 'mem', spli...  9.42 us
    dynamic_slice x8, local copies, waits for them, and re-layouts, attend_slots(): lax.map(one_group, (grouped_queries, grouped_blocks))  8.38 us
    scatter x1, local copies, waits for them, and re-layouts, per_device(): jnp.zeros((devices_mem * capacity, row_width), jnp.bfloat16).at[position]  7.73 us
  transfers between devices with their start and end apart: 7, of which 5 were waited for; matrix products, arithmetic and copies ran while one was open for 12% of the time, Pallas kernels for 0%

commit v1 on v0

v1 whole, which is shorter than its diff:
```python
import functools
import math

import jax
import jax.numpy as jnp
from jax import lax
from jax.experimental import pallas as pl
from jax.experimental.pallas import tpu as pltpu
from jax.sharding import PartitionSpec as P

MESH = pl.DeviceIdType.MESH
NEG = -1e30
LOG2E = 1.4426950408889634


def ring_order(i):
    return i + (i // 2) * (1 - 2 * (i % 2))


def kernel(
    side, heads_n, scale,
    q_hbm, kv_hbm, sel_hbm, cnt_hbm, w_hbm,
    out_ref, heat_ref,
    qin, qout, sin, sout, kv, cnt, w,
    meta_v, meta_s, own, own_ml, part, part_ml, sib, sib_ml, comb, comb_ml, ret, ret_ml,
    att, ysend, yrecv,
    lsem, msem,
    in_s, in_r, fw_s, fw_r, sb_s, sb_r, rt_s, rt_r, y_s, y_r,
):
    n = side * side
    reqs, heads = q_hbm.shape[0], q_hbm.shape[1]
    dim = q_hbm.shape[2]
    blocks = kv.shape[0]
    tok = kv.shape[2]
    group = heads // 2
    me = lax.axis_index("mem")
    y = lax.axis_index("head")
    core = me % 2
    chip = me // 2
    cx, cz = chip // side, chip % side
    sibling = me + 1 - 2 * core

    def at(k, sign):
        dx, dz = k // side, k % side
        if side == 4:
            dx, dz = ring_order(dx), ring_order(dz)
        px = (cx + sign * dx + side) % side
        pz = (cz + sign * dz + side) % side
        return (px * side + pz) * 2 + core

    def remote(src, dst, ss, rs, **device):
        return pltpu.make_async_remote_copy(
            src_ref=src, dst_ref=dst, send_sem=ss, recv_sem=rs,
            device_id=device, device_id_type=MESH,
        )

    loc = [
        pltpu.make_async_copy(sel_hbm, sin.at[0], lsem.at[0]),
        pltpu.make_async_copy(q_hbm, qin.at[0], lsem.at[1]),
        pltpu.make_async_copy(kv_hbm, kv, lsem.at[2]),
        pltpu.make_async_copy(cnt_hbm, cnt, lsem.at[3]),
    ]
    for c in loc:
        c.start()

    barrier = pltpu.get_barrier_semaphore()
    pl.semaphore_signal(barrier, inc=1, device_id={"mem": sibling}, device_id_type=MESH)

    @pl.loop(1, n)
    def _(k):
        pl.semaphore_signal(barrier, inc=1, device_id={"mem": at(k, 1)}, device_id_type=MESH)

    for j in range(1, heads_n):
        pl.semaphore_signal(
            barrier, inc=1, device_id={"head": (y + j) % heads_n}, device_id_type=MESH
        )
    pl.semaphore_wait(barrier, n + heads_n - 1)

    def fw(k, stream, from_hbm=False):
        src, dst = ((sin, sout), (qin, qout))[stream]
        src = (sel_hbm, q_hbm)[stream] if from_hbm else src.at[k]
        return remote(src, dst.at[k], fw_s.at[stream, k], fw_r.at[stream, k], mem=sibling)

    def plane(k, stream):
        src, dst = ((sel_hbm, sin), (q_hbm, qin))[stream]
        return remote(src, dst.at[k], in_s.at[stream, k], in_r.at[stream, k], mem=at(k, 1))

    for s in range(2):
        fw(0, s, True).start()

    @pl.loop(1, n)
    def _(k):
        for s in range(2):
            plane(k, s).start()

    wcopies = [
        pltpu.make_async_copy(
            w_hbm.at[:, pl.ds(pl.multiple_of(((y + j) % heads_n) * out_ref.shape[1], 128), out_ref.shape[1])],
            w.at[j], lsem.at[4 + j],
        )
        for j in range(heads_n)
    ]
    for c in wcopies:
        c.start()

    row = lax.broadcasted_iota(jnp.int32, (heads, 2 * tok // 2), 0)
    lane = lax.broadcasted_iota(jnp.int32, (heads, 2 * tok // 2), 1)
    kmask = (row // group) == (lane // (tok // 2))
    lane_r = lax.broadcasted_iota(jnp.int32, (reqs, 128), 1)
    row_r = lax.broadcasted_iota(jnp.int32, (reqs, 128), 0)
    lane_h = lax.broadcasted_iota(jnp.int32, (heads, 128), 1)
    c2 = scale * LOG2E

    def table(sel_ref, slot, k, hits):
        sel = sel_ref[k]
        here = (sel // blocks) == me
        local = sel % blocks
        first = jnp.min(jnp.where(here, local, blocks), axis=1, keepdims=True)
        last = jnp.max(jnp.where(here, local, -1), axis=1, keepdims=True)
        b0 = jnp.broadcast_to(jnp.where(first < blocks, first, -1), (reqs, 128))
        b1 = jnp.broadcast_to(jnp.where(last > first, last, -1), (reqs, 128))
        hits = hits + (b0 == lane_r).astype(jnp.float32) + (b1 == lane_r).astype(jnp.float32)
        line = jnp.where(lane_r == row_r, b0, 0) + jnp.where(lane_r == row_r + reqs, b1, 0)
        meta_v[slot, k] = jnp.sum(line, axis=0, keepdims=True)
        pltpu.make_async_copy(meta_v.at[slot, k], meta_s.at[slot, k], msem.at[slot, k]).start()
        return hits

    def attend(q_ref, slot, k, emit):
        pltpu.make_async_copy(meta_v.at[slot, k], meta_s.at[slot, k], msem.at[slot, k]).wait()
        ml = jnp.zeros((heads, 128), jnp.float32)
        for r in range(reqs):
            b0 = meta_s[slot, k, 0, r]
            b1 = meta_s[slot, k, 0, reqs + r]
            i0, i1 = jnp.maximum(b0, 0), jnp.maximum(b1, 0)
            off0 = jnp.where(b0 < 0, NEG, 0.0)
            off1 = jnp.where(b1 < 0, NEG, 0.0)
            q = q_ref[k, r]
            dims = (((1,), (1,)), ((), ()))
            s0 = lax.dot_general(q, kv[i0, 0], dims, preferred_element_type=jnp.float32)
            s1 = lax.dot_general(q, kv[i1, 0], dims, preferred_element_type=jnp.float32)
            s0 = jnp.where(kmask, s0 + off0, NEG)
            s1 = jnp.where(kmask, s1 + off1, NEG)
            m = jnp.max(jnp.maximum(s0, s1), axis=1, keepdims=True)
            p0 = jnp.exp2((s0 - m) * c2)
            p1 = jnp.exp2((s1 - m) * c2)
            l = jnp.sum(p0 + p1, axis=1, keepdims=True)
            o = jnp.dot(p0.astype(jnp.bfloat16), kv[i0, 1], preferred_element_type=jnp.float32)
            o += jnp.dot(p1.astype(jnp.bfloat16), kv[i1, 1], preferred_element_type=jnp.float32)
            emit(r, o)
            ml = jnp.where(lane_h == r, m, ml)
            ml = jnp.where(lane_h == reqs + r, l, ml)
        return ml

    def to_sibling(k):
        return (
            remote(part.at[k], sib.at[k], sb_s.at[0, k], sb_r.at[0, k], mem=sibling),
            remote(part_ml.at[k], sib_ml.at[k], sb_s.at[1, k], sb_r.at[1, k], mem=sibling),
        )

    def to_owner(k):
        return (
            remote(comb.at[k], ret.at[k], rt_s.at[0, k], rt_r.at[0, k], mem=at(k, -1)),
            remote(comb_ml.at[k], ret_ml.at[k], rt_s.at[1, k], rt_r.at[1, k], mem=at(k, -1)),
        )

    loc[0].wait()
    loc[1].wait()
    loc[2].wait()

    def step(t, hits):
        def arrive_in(hits):
            @pl.when(t > 0)
            def _():
                for s in range(2):
                    plane(t, s).wait_recv()
                    fw(t, s).start()
            return table(sin, 0, t, hits)

        hits = lax.cond(t < n, arrive_in, lambda h: h, hits)

        def arrive_out(hits):
            for s in range(2):
                fw(t - 1, s).wait_recv()
            return table(sout, 1, t - 1, hits)

        hits = lax.cond((t >= 1) & (t - 1 < n), arrive_out, lambda h: h, hits)

        @pl.when((t >= 2) & (t - 2 < n))
        def _():
            k = t - 2

            def emit_part(r, o):
                part[k, r] = o.astype(jnp.bfloat16)

            part_ml[k] = attend(qout, 1, k, emit_part)

            def emit_own(r, o):
                own[k, r] = o

            own_ml[k] = attend(qin, 0, k, emit_own)
            for c in to_sibling(k):
                c.start()

        @pl.when(t >= 4)
        def _():
            k = t - 4
            for c in to_sibling(k):
                c.wait_recv()
            a, b = own_ml[k], sib_ml[k]
            top = jnp.maximum(a, b)
            fa, fb = jnp.exp2((a - top) * c2), jnp.exp2((b - top) * c2)
            total = pltpu.roll(fa, reqs, 1) * a + pltpu.roll(fb, reqs, 1) * b
            comb_ml[k] = jnp.where(lane_h < reqs, top, total)
            for r in range(reqs):
                o = own[k, r] * fa[:, r : r + 1] + sib[k, r].astype(jnp.float32) * fb[:, r : r + 1]
                comb[k, r] = o.astype(jnp.bfloat16)

            @pl.when(k > 0)
            def _():
                for c in to_owner(k):
                    c.start()

        return hits

    hits = lax.fori_loop(0, n + 4, step, jnp.zeros((reqs, 128), jnp.float32))

    loc[3].wait()
    counts = cnt[...].astype(jnp.float32)
    decay = jnp.exp2(-lax.broadcasted_iota(jnp.int32, counts.shape, 0).astype(jnp.float32))
    heat_ref[...] = (
        jnp.sum(decay * counts, axis=0, keepdims=True)
        + jnp.sum(hits, axis=0, keepdims=True)[:, : counts.shape[1]]
    )

    ret[0] = comb[0]
    ret_ml[0] = comb_ml[0]

    @pl.loop(1, n)
    def _(k):
        for c in to_owner(k):
            c.wait_recv()

    top = ret_ml[0]
    for k in range(1, n):
        top = jnp.maximum(top, ret_ml[k])
    den = jnp.zeros((heads, 128), jnp.float32)
    for k in range(n):
        f = jnp.exp2((ret_ml[k] - top) * c2)
        den += f * pltpu.roll(ret_ml[k], 128 - reqs, 1)
    inv = 1.0 / den
    for r in range(reqs):
        att[r] = jnp.zeros((heads, dim), jnp.float32)

    @pl.loop(0, n)
    def _(k):
        f = jnp.exp2((ret_ml[k] - top) * c2) * inv
        for r in range(reqs):
            att[r] += ret[k, r].astype(jnp.float32) * f[:, r : r + 1]

    lhs = jnp.concatenate(
        [att[:, h, :].astype(jnp.bfloat16) for h in range(heads)], axis=1
    )

    for c in wcopies:
        c.wait()

    def y_copy(j):
        return remote(ysend.at[j], yrecv.at[j], y_s.at[j], y_r.at[j], head=(y + j) % heads_n)

    for j in range(1, heads_n):
        ysend[j] = jnp.dot(lhs, w[j], preferred_element_type=jnp.float32).astype(jnp.bfloat16)
        y_copy(j).start()
    total = jnp.dot(lhs, w[0], preferred_element_type=jnp.float32).astype(jnp.bfloat16).astype(jnp.float32)
    for j in range(1, heads_n):
        y_copy(j).wait()
        total += yrecv[j].astype(jnp.float32)
    out_ref[...] = total.astype(out_ref.dtype)

    for s in range(2):
        fw(0, s, True).wait_send()

    @pl.loop(0, n)
    def _(k):
        for c in to_sibling(k):
            c.wait_send()

        @pl.when(k > 0)
        def _():
            for s in range(2):
                fw(k, s).wait_send()
                plane(k, s).wait_send()
            for c in to_owner(k):
                c.wait_send()


def per_device(side, heads_n, queries, cache_blocks, selected, counts, output_weight):
    reqs, heads, dim = queries.shape
    blocks = cache_blocks.shape[0]
    tok = cache_blocks.shape[2] * cache_blocks.shape[3]
    kv = cache_blocks.reshape(blocks, 2, tok, dim)
    n = side * side
    cols = output_weight.shape[1] // heads_n
    bf, f32, i32 = jnp.bfloat16, jnp.float32, jnp.int32
    any_ = pl.BlockSpec(memory_space=pl.ANY)
    vmem = pl.BlockSpec(memory_space=pltpu.VMEM)
    dma = pltpu.SemaphoreType.DMA
    out, heat = pl.pallas_call(
        functools.partial(kernel, side, heads_n, dim ** -0.5),
        out_shape=(
            jax.ShapeDtypeStruct((reqs, cols), bf),
            jax.ShapeDtypeStruct((1, blocks), f32),
        ),
        in_specs=[any_] * 5,
        out_specs=(vmem, vmem),
        scratch_shapes=[
            pltpu.VMEM((n, reqs, heads, dim), bf),
            pltpu.VMEM((n, reqs, heads, dim), bf),
            pltpu.VMEM((n,) + selected.shape, i32),
            pltpu.VMEM((n,) + selected.shape, i32),
            pltpu.VMEM(kv.shape, bf),
            pltpu.VMEM(counts.shape, i32),
            pltpu.VMEM((heads_n, output_weight.shape[0], cols), bf),
            pltpu.VMEM((2, n, 1, 128), i32),
            pltpu.SMEM((2, n, 1, 128), i32),
            pltpu.VMEM((n, reqs, heads, dim), f32),
            pltpu.VMEM((n, heads, 128), f32),
            pltpu.VMEM((n, reqs, heads, dim), bf),
            pltpu.VMEM((n, heads, 128), f32),
            pltpu.VMEM((n, reqs, heads, dim), bf),
            pltpu.VMEM((n, heads, 128), f32),
            pltpu.VMEM((n, reqs, heads, dim), bf),
            pltpu.VMEM((n, heads, 128), f32),
            pltpu.VMEM((n, reqs, heads, dim), bf),
            pltpu.VMEM((n, heads, 128), f32),
            pltpu.VMEM((reqs, heads, dim), f32),
            pltpu.VMEM((heads_n, reqs, cols), bf),
            pltpu.VMEM((heads_n, reqs, cols), bf),
            dma((4 + heads_n,)), dma((2, n)),
            dma((2, n)), dma((2, n)), dma((2, n)), dma((2, n)),
            dma((2, n)), dma((2, n)), dma((2, n)), dma((2, n)),
            dma((heads_n,)), dma((heads_n,)),
        ],
        compiler_params=pltpu.CompilerParams(collective_id=0, has_side_effects=True),
    )(queries, kv, selected, counts, output_weight)
    return out, heat.reshape(blocks)


def solution(mesh):
    side = math.isqrt(mesh.shape["mem"] // 2)
    return jax.shard_map(
        functools.partial(per_device, side, mesh.shape["head"]),
        mesh=mesh,
        in_specs=(
            P("mem", "head", None),
            P("mem", None, "head", None, None),
            P("mem", None),
            P(None, "mem"),
            P("head", None),
        ),
        out_specs=(P("mem", "head"), P("mem")),
        check_vma=False,
    )
```

time: 224 us -> 176 us (0.79)
  Pallas kernels: 0 us -> 171 us
  waiting for transfers between devices: 64.3 us -> 0 us
  matrix products: 49 us -> 0 us
  starting transfers between devices: 37 us -> 0 us
  local copies, waits for them, and re-layouts: 32.1 us -> 2.55 us
  other arithmetic: 24.1 us -> 0 us
  between operations: 14.3 us -> 0.64 us
    pallas_call x0 -> x1, Pallas kernels: none -> 171 us  [per_device(): pl.pallas_call(functools.partial(kernel, side, heads_n, dim ** (-0.5)), o...]
    all_to_all x6 -> x0, waiting for transfers between devices: 64.3 us -> none  [the longest x1 25.8 us: per_device(): lax.all_to_all(source_outputs, 'mem', split_axis=0, concat_axis=0, tiled=...]
    dot_general x18 -> x0, matrix products: 49 us -> none  [the longest x8 26.8 us: resident_partial(): jnp.einsum('shgbt,bhtd->shgd', weights, value_rows, preferred_element_typ...]
    all_to_all x6 -> x0, starting transfers between devices: 36.8 us -> none  [the longest x1 9.42 us: per_device(): lax.all_to_all(send_labels.reshape(devices_mem, capacity, 2), 'mem', spli...]
    reduce_sum x14 -> x0, other arithmetic: 15.8 us -> none  [the longest x8 13.5 us: resident_partial(): totals = jnp.sum(expo_terms, axis=(-2, -1))]
    scatter x2 -> x0, local copies, waits for them, and re-layouts: 9.56 us -> none  [the longest x1 7.73 us: per_device(): jnp.zeros((devices_mem * capacity, row_width), jnp.bfloat16).at[position]]
    dynamic_slice x8 -> x0, local copies, waits for them, and re-layouts: 8.38 us -> none  [attend_slots(): lax.map(one_group, (grouped_queries, grouped_blocks))]
    scatter-add x1 -> x0, other arithmetic: 4.09 us -> none  [per_device(): jnp.zeros((devices_mem * blocks_each,), jnp.float32).at[flat_ids].add(1.0)]
  transfers between devices with their start and end apart: 7 -> 0, of which waited for: 5 -> 0; matrix products, arithmetic and copies ran while one was open for 12% -> 0% of each run, Pallas kernels for 0% -> 0%
where the time goes in v1:
time: 176 us; the launch traced here: 175 us
  Pallas kernels  171 us (97%)
  local copies, waits for them, and re-layouts  2.55 us (1%)
    pallas_call x1, Pallas kernels, per_device(): pl.pallas_call(functools.partial(kernel, side, heads_n, dim ** (-0.5)), o...  171 us

profile of v1, /device:TPU:1, one launch (start us, length us, event | category | flops | bytes accessed | tf_op | source)
XLA Modules:
  0.0 174.5 jit_solution(6677759209790733910)
XLA Ops:
  0.6 171.3 %shard_map.68 = (bf16[16,1024]{1,0:T(8,128)(2,1)}, f32[1,32]{1,0:T(1,128)}) custom-call(bf16[16,8,128]{2,1,0:T(8,128)(2,1)} %q_hbm.1, bf16[32,2,128,128]{3,2,1,0:T(8,128)(2,1)} %bitcast.2, s32[16,32]{1,0:T(8,128)} %sel_hbm.1, s32[16,32]{1,0:T(8,128)} %cnt_hbm.1, bf16[1024,4096]{1,0:T(8,128)(2,1)} %w_hbm.1), custom_call_target="tpu_custom_call" | custom-call | tf_op jit(solution)/shard_map/pallas_call | solution.py:307
  172.0 1.4 copy.9
  173.4 1.2 copy.10

commit v2 on v1

v2 whole, which is shorter than its diff:
```python
import functools
import math

import jax
import jax.numpy as jnp
from jax import lax
from jax.experimental import pallas as pl
from jax.experimental.pallas import tpu as pltpu
from jax.sharding import PartitionSpec as P

MESH = pl.DeviceIdType.MESH
NEG = -1e30
LOG2E = 1.4426950408889634


def offsets_in_order(side):
    far = list(range(2, side - 1))
    near = [1] + ([side - 1] if side > 2 else [])
    row = near + far
    order = [(0, 0)] + [(dx, 0) for dx in row]
    for dz in far:
        order += [(dx, dz) for dx in [0] + row]
    order += [(dx, dz) for dx in row for dz in near]
    return order + [(0, dz) for dz in near]


def kernel(
    side, heads_n, scale, later,
    q_hbm, kv_hbm, sel_hbm, cnt_hbm, w_hbm,
    out_ref, heat_ref,
    qin, qout, tin, tout, town, sel_v, kv, kt, cnt, w, hits,
    meta_s, p_in, p_out, own, own_ml, part, part_ml, sib, sib_ml, comb, comb_ml, ret, ret_ml,
    att, ysend, yrecv,
    lsem, msem,
    in_s, in_r, fw_s, fw_r, sb_s, sb_r, rt_s, rt_r, y_s, y_r,
):
    bf, f32, i32 = jnp.bfloat16, jnp.float32, jnp.int32
    n = side * side
    order = offsets_in_order(side)
    reqs, heads, dim = q_hbm.shape
    blocks, tok = kv.shape[0], kv.shape[2]
    group = heads // 2
    cols = out_ref.shape[1]
    me = lax.axis_index("mem")
    y = lax.axis_index("head")
    core = me % 2
    chip = me // 2
    cx, cz = chip // side, chip % side
    sibling = me + 1 - 2 * core
    line = cz * 2 + core
    c2 = scale * LOG2E

    def chip_at(dx, dz):
        px = (cx + dx + side) % side
        pz = (cz + dz + side) % side
        return (px * side + pz) * 2 + core

    def pick(values, k):
        if isinstance(k, int):
            return values[k]
        found = i32(values[0])
        for i in range(1, n):
            found = jnp.where(k == i, i32(values[i]), found)
        return found

    def remote(src, dst, ss, rs, **device):
        return pltpu.make_async_remote_copy(
            src_ref=src, dst_ref=dst, send_sem=ss, recv_sem=rs,
            device_id=device, device_id_type=MESH,
        )

    def fw(k, stream, first=False):
        src, dst = ((tin, tout), (qin, qout))[stream]
        src = (town.at[cx], q_hbm)[stream] if first else src.at[k]
        return remote(src, dst.at[k], fw_s.at[stream, k], fw_r.at[stream, k], mem=sibling)

    def plane(k, stream):
        dx, dz = order[k]
        dst = (tin, qin)[stream]
        if dz == 0:
            src = (town.at[(cx + dx) % side], q_hbm)[stream]
            peer = chip_at(dx, 0)
        elif dx == 0:
            src = (town.at[cx], q_hbm)[stream]
            peer = chip_at(0, dz)
        else:
            src = dst.at[order.index((dx, 0))]
            peer = chip_at(0, dz)
        return remote(src, dst.at[k], in_s.at[stream, k], in_r.at[stream, k], mem=peer)

    def arrived(k, stream):
        dst = (tin, qin)[stream]
        return remote(dst.at[k], dst.at[k], in_s.at[stream, k], in_r.at[stream, k], mem=sibling)

    def meta(k, slot):
        src = (tin, tout)[slot]
        return pltpu.make_async_copy(
            src.at[k, pl.ds(line, 1)], meta_s.at[slot, k], msem.at[slot, k]
        )

    def to_sibling(k):
        return (
            remote(part.at[k], sib.at[k], sb_s.at[0, k], sb_r.at[0, k], mem=sibling),
            remote(part_ml.at[k], sib_ml.at[k], sb_s.at[1, k], sb_r.at[1, k], mem=sibling),
        )

    def to_owner(k):
        peer = chip_at(-pick([d[0] for d in order], k), -pick([d[1] for d in order], k))
        return (
            remote(comb.at[k], ret.at[k], rt_s.at[0, k], rt_r.at[0, k], mem=peer),
            remote(comb_ml.at[k], ret_ml.at[k], rt_s.at[1, k], rt_r.at[1, k], mem=peer),
        )

    loc = [
        pltpu.make_async_copy(sel_hbm, sel_v, lsem.at[0]),
        pltpu.make_async_copy(kv_hbm, kv, lsem.at[1]),
        pltpu.make_async_copy(q_hbm, qin.at[0], lsem.at[2]),
        pltpu.make_async_copy(cnt_hbm, cnt, lsem.at[3]),
    ]
    for c in loc:
        c.start()

    barrier = pltpu.get_barrier_semaphore()
    pl.semaphore_signal(barrier, inc=1, device_id={"mem": sibling}, device_id_type=MESH)
    for d in range(1, side):
        for peer in (chip_at(d, 0), chip_at(0, d)):
            pl.semaphore_signal(barrier, inc=1, device_id={"mem": peer}, device_id_type=MESH)
    for j in range(1, heads_n):
        pl.semaphore_signal(
            barrier, inc=1, device_id={"head": (y + j) % heads_n}, device_id_type=MESH
        )

    devices = 2 * n
    loc[0].wait()
    sel = sel_v[...]
    target, local = sel // blocks, sel % blocks
    dev = lax.broadcasted_iota(i32, (devices, sel.shape[1]), 0)
    lane_d = lax.broadcasted_iota(i32, (devices, 128), 1)
    table = jnp.full((devices, 128), -1, i32)
    for r in range(reqs):
        here = target[r : r + 1] == dev
        value = jnp.broadcast_to(local[r : r + 1], dev.shape)
        first = jnp.min(jnp.where(here, value, blocks), axis=1, keepdims=True)
        last = jnp.max(jnp.where(here, value, -1), axis=1, keepdims=True)
        table = jnp.where((lane_d == r) & (first < blocks), first, table)
        table = jnp.where((lane_d == reqs + r) & (last > first), last, table)
    for d in range(side):
        town[d] = table[d * 2 * side : (d + 1) * 2 * side]
    tin[0] = town[cx]
    meta(0, 0).start()

    pl.semaphore_wait(barrier, 2 * (side - 1) + heads_n)

    for k in list(range(1, side)) + [i for i in range(n) if i and order[i][0] == 0]:
        for s in range(2):
            plane(k, s).start()
    for s in range(2):
        fw(0, s, True).start()

    wcopies = [
        pltpu.make_async_copy(
            w_hbm.at[:, pl.ds(pl.multiple_of(((y + j) % heads_n) * cols, 128), cols)],
            w.at[j], lsem.at[4 + j],
        )
        for j in range(heads_n)
    ]
    for c in wcopies:
        c.start()

    row = lax.broadcasted_iota(i32, (heads, tok), 0)
    lane = lax.broadcasted_iota(i32, (heads, tok), 1)
    kmask = (row // group) == (lane // (tok // 2))
    lane_h = lax.broadcasted_iota(i32, (heads, 128), 1)
    brow = lax.broadcasted_iota(i32, (blocks, 128), 0)
    zero = jnp.zeros((heads, dim), bf)

    def four(a, b, c, d):
        return jnp.concatenate(
            [jnp.concatenate([a, b], axis=1), jnp.concatenate([c, d], axis=1)], axis=0
        )

    def softmax(s0, s1, off0, off1):
        s0 = jnp.where(kmask, s0 + off0, NEG)
        s1 = jnp.where(kmask, s1 + off1, NEG)
        m = jnp.max(jnp.maximum(s0, s1), axis=1, keepdims=True)
        p0, p1 = jnp.exp2((s0 - m) * c2), jnp.exp2((s1 - m) * c2)
        return p0, p1, m, jnp.sum(p0 + p1, axis=1, keepdims=True)

    def scores(q_ref, slot, k, p_ref, ml_ref):
        ml = jnp.zeros((heads, 128), f32)
        for r in range(0, reqs, 2):
            ids = [meta_s[slot, k, 0, i] for i in (r, reqs + r, r + 1, reqs + r + 1)]
            off = [jnp.where(b < 0, NEG, 0.0) for b in ids]
            k0, k1, k2, k3 = [kt[jnp.maximum(b, 0)] for b in ids]
            lhs = four(q_ref[k, r], zero, zero, q_ref[k, r + 1])
            s = jnp.dot(lhs, four(k0, k1, k2, k3), preferred_element_type=f32)
            a0, a1, ma, la = softmax(s[:heads, :tok], s[:heads, tok:], off[0], off[1])
            b0, b1, mb, lb = softmax(s[heads:, :tok], s[heads:, tok:], off[2], off[3])
            p_ref[r // 2] = jnp.concatenate(
                [jnp.concatenate([a0, b0], axis=0).astype(bf), jnp.concatenate([a1, b1], axis=0).astype(bf)],
                axis=1,
            )
            for i, v in ((r, ma), (reqs + r, la), (r + 1, mb), (reqs + r + 1, lb)):
                ml = jnp.where(lane_h == i, v, ml)
        ml_ref[k] = ml

    def values(slot, k, p_list, emit):
        for r in range(0, reqs, 2):
            ids = [meta_s[slot, k, 0, i] for i in (r, reqs + r, r + 1, reqs + r + 1)]
            v0, v1, v2, v3 = [kv[jnp.maximum(b, 0), 1] for b in ids]
            o = jnp.dot(p_list[r // 2], four(v0, v2, v1, v3), preferred_element_type=f32)
            emit(k, r, o[:heads, :dim])
            emit(k, r + 1, o[heads:, dim:])

    def emit_own(k, r, o):
        own[k, r] = o

    def emit_part(k, r, o):
        part[k, r] = o.astype(bf)

    def load(p_ref):
        return [p_ref[i] for i in range(reqs // 2)]

    def count(k):
        for t in (tin, tout):
            hits[...] += jnp.where(t[k, pl.ds(line, 1)] == brow, 1.0, 0.0)

    def combine(k):
        a, b = own_ml[k], sib_ml[k]
        top = jnp.maximum(a, b)
        fa, fb = jnp.exp2((a - top) * c2), jnp.exp2((b - top) * c2)
        total = pltpu.roll(fa, reqs, 1) * a + pltpu.roll(fb, reqs, 1) * b
        comb_ml[k] = jnp.where(lane_h < reqs, top, total)
        for r in range(reqs):
            o = own[k, r] * fa[:, r : r + 1] + sib[k, r].astype(f32) * fb[:, r : r + 1]
            comb[k, r] = o.astype(bf)

    def send_owner(k):
        for c in to_owner(k):
            c.start()

    loc[1].wait()

    @pl.loop(0, blocks // 4)
    def _(b):
        for i in range(4):
            kt[b * 4 + i] = kv[b * 4 + i, 0].T

    hits[...] = jnp.zeros(hits.shape, f32)
    loc[2].wait()
    meta(0, 0).wait()
    scores(qin, 0, 0, p_in, own_ml)

    for k in range(1, side):
        for s in range(2):
            arrived(k, s).wait_recv()
            for i in range(n):
                if order[i][0] == order[k][0] and order[i][1]:
                    plane(i, s).start()
            fw(k, s).start()
        meta(k, 0).start()

    for s in range(2):
        fw(0, s).wait_recv()
    meta(0, 1).start()
    meta(0, 1).wait()
    scores(qout, 1, 0, p_out, part_ml)
    values(1, 0, load(p_out), emit_part)
    for c in to_sibling(0):
        c.start()
    count(0)
    fw(1, 0).wait_recv()
    meta(1, 1).start()

    @pl.loop(1, n)
    def _(t):
        ahead = t + side - 1

        @pl.when(ahead < n)
        def _():
            for s in range(2):
                arrived(ahead, s).wait_recv()
                fw(ahead, s).start()
            meta(ahead, 0).start()

        @pl.when(t + 1 < n)
        def _():
            fw(t + 1, 0).wait_recv()
            meta(t + 1, 1).start()

        @pl.when(t >= 2)
        def _():
            for c in to_sibling(t - 2):
                c.wait_recv()

        fw(t, 1).wait_recv()
        meta(t, 0).wait()
        meta(t, 1).wait()

        p = load(p_in)
        scores(qout, 1, t, p_out, part_ml)
        values(0, t - 1, p, emit_own)
        p = load(p_out)
        scores(qin, 0, t, p_in, own_ml)
        values(1, t, p, emit_part)
        count(t)
        for c in to_sibling(t):
            c.start()

        @pl.when(t >= 2)
        def _():
            combine(t - 2)

        @pl.when(t >= 3)
        def _():
            send_owner(t - 2)

    values(0, n - 1, load(p_in), emit_own)
    for k in (n - 2, n - 1):
        for c in to_sibling(k):
            c.wait_recv()
        combine(k)
        send_owner(k)

    loc[3].wait()
    counts = cnt[...].astype(f32)
    decay = jnp.exp2(-lax.broadcasted_iota(i32, counts.shape, 0).astype(f32))
    here = jnp.broadcast_to(jnp.sum(hits[...], axis=1, keepdims=True), (blocks, blocks))
    eye = lax.broadcasted_iota(i32, (blocks, blocks), 0) == lax.broadcasted_iota(i32, (blocks, blocks), 1)
    heat_ref[...] = jnp.sum(decay * counts, axis=0, keepdims=True) + jnp.sum(
        jnp.where(eye, here, 0.0), axis=0, keepdims=True
    )

    ret[0] = comb[0]
    ret_ml[0] = comb_ml[0]

    def merged(start, stop):
        @pl.loop(max(start, 1), stop)
        def _(k):
            for c in to_owner(k):
                c.wait_recv()

        top = ret_ml[start]
        for k in range(start + 1, stop):
            top = jnp.maximum(top, ret_ml[k])
        den = jnp.zeros((heads, 128), f32)
        acc = [jnp.zeros((heads, dim), f32)] * reqs

        def add(k, carry):
            den, acc = carry
            f = jnp.exp2((ret_ml[k] - top) * c2)
            den += f * pltpu.roll(ret_ml[k], 128 - reqs, 1)
            return den, [acc[r] + ret[k, r].astype(f32) * f[:, r : r + 1] for r in range(reqs)]

        den, acc = lax.fori_loop(start, stop, add, (den, acc))
        return top, den, acc

    top_a, den_a, acc_a = merged(0, n - later)
    top_b, den_b, acc_b = merged(n - later, n)
    top = jnp.maximum(top_a, top_b)
    fa, fb = jnp.exp2((top_a - top) * c2), jnp.exp2((top_b - top) * c2)
    inv = 1.0 / (fa * den_a + fb * den_b)
    fa, fb = fa * inv, fb * inv
    for r in range(reqs):
        att[r] = acc_a[r] * fa[:, r : r + 1] + acc_b[r] * fb[:, r : r + 1]

    lhs = jnp.concatenate([att[:, h, :].astype(bf) for h in range(heads)], axis=1)

    for c in wcopies:
        c.wait()

    def y_copy(j):
        return remote(ysend.at[j], yrecv.at[j], y_s.at[j], y_r.at[j], head=(y + j) % heads_n)

    for j in range(1, heads_n):
        ysend[j] = jnp.dot(lhs, w[j], preferred_element_type=f32).astype(bf)
        y_copy(j).start()
    total = jnp.dot(lhs, w[0], preferred_element_type=f32).astype(bf).astype(f32)
    for j in range(1, heads_n):
        y_copy(j).wait()
        total += yrecv[j].astype(f32)
    out_ref[...] = total.astype(out_ref.dtype)

    for s in range(2):
        fw(0, s, True).wait_send()
        for k in range(1, n):
            plane(k, s).wait_send()

    @pl.loop(0, n)
    def _(k):
        for c in to_sibling(k):
            c.wait_send()

        @pl.when(k > 0)
        def _():
            for s in range(2):
                fw(k, s).wait_send()
            for c in to_owner(k):
                c.wait_send()


def per_device(side, heads_n, queries, cache_blocks, selected, counts, output_weight):
    reqs, heads, dim = queries.shape
    blocks = cache_blocks.shape[0]
    tok = cache_blocks.shape[2] * cache_blocks.shape[3]
    kv = cache_blocks.reshape(blocks, 2, tok, dim)
    n = side * side
    cols = output_weight.shape[1] // heads_n
    bf, f32, i32 = jnp.bfloat16, jnp.float32, jnp.int32
    any_ = pl.BlockSpec(memory_space=pl.ANY)
    vmem = pl.BlockSpec(memory_space=pltpu.VMEM)
    dma = pltpu.SemaphoreType.DMA
    rows = pltpu.VMEM((n, reqs, heads, dim), bf)
    small = pltpu.VMEM((n, heads, 128), f32)
    tiles = pltpu.VMEM((n, 2 * side, 128), i32)
    out, heat = pl.pallas_call(
        functools.partial(kernel, side, heads_n, dim ** -0.5, max(2, n // 4)),
        out_shape=(
            jax.ShapeDtypeStruct((reqs, cols), bf),
            jax.ShapeDtypeStruct((1, blocks), f32),
        ),
        in_specs=[any_] * 5,
        out_specs=(vmem, vmem),
        scratch_shapes=[
            rows, rows, tiles, tiles,
            pltpu.VMEM((side, 2 * side, 128), i32),
            pltpu.VMEM(selected.shape, i32),
            pltpu.VMEM(kv.shape, bf),
            pltpu.VMEM((blocks, dim, tok), bf),
            pltpu.VMEM(counts.shape, i32),
            pltpu.VMEM((heads_n, output_weight.shape[0], cols), bf),
            pltpu.VMEM((blocks, 128), f32),
            pltpu.SMEM((2, n, 1, 128), i32),
            pltpu.VMEM((reqs // 2, 2 * heads, 2 * tok), bf),
            pltpu.VMEM((reqs // 2, 2 * heads, 2 * tok), bf),
            pltpu.VMEM((n, reqs, heads, dim), f32),
            small, rows, small, rows, small, rows, small, rows, small,
            pltpu.VMEM((reqs, heads, dim), f32),
            pltpu.VMEM((heads_n, reqs, cols), bf),
            pltpu.VMEM((heads_n, reqs, cols), bf),
            dma((4 + heads_n,)), dma((2, n)),
            dma((2, n)), dma((2, n)), dma((2, n)), dma((2, n)),
            dma((2, n)), dma((2, n)), dma((2, n)), dma((2, n)),
            dma((heads_n,)), dma((heads_n,)),
        ],
        compiler_params=pltpu.CompilerParams(collective_id=0, has_side_effects=True),
    )(queries, kv, selected, counts, output_weight)
    return out, heat.reshape(blocks)


def solution(mesh):
    side = math.isqrt(mesh.shape["mem"] // 2)
    return jax.shard_map(
        functools.partial(per_device, side, mesh.shape["head"]),
        mesh=mesh,
        in_specs=(
            P("mem", "head", None),
            P("mem", None, "head", None, None),
            P("mem", None),
            P(None, "mem"),
            P("head", None),
        ),
        out_specs=(P("mem", "head"), P("mem")),
        check_vma=False,
    )
```

time: 176 us -> 44.7 us (0.25)
  Pallas kernels: 171 us -> 41.3 us
    pallas_call x1, Pallas kernels: 171 us -> 41.3 us  [per_device(): pl.pallas_call(functools.partial(kernel, side, heads_n, dim ** (-0.5), ma...]
where the time goes in v2:
time: 44.7 us; the launch traced here: 44.5 us
  Pallas kernels  41.3 us (92%)
  local copies, waits for them, and re-layouts  2.55 us (6%)
  between operations  0.64 us (1%)
    pallas_call x1, Pallas kernels, per_device(): pl.pallas_call(functools.partial(kernel, side, heads_n, dim ** (-0.5), ma...  41.3 us
    unnamed x2, local copies, waits for them, and re-layouts  2.55 us

profile of v2, /device:TPU:1, one launch (start us, length us, event | category | flops | bytes accessed | tf_op | source)
XLA Modules:
  0.0 44.5 jit_solution(18021575000455750829)
XLA Ops:
  0.6 41.3 %shard_map.68 = (bf16[16,1024]{1,0:T(8,128)(2,1)}, f32[1,32]{1,0:T(1,128)}) custom-call(bf16[16,8,128]{2,1,0:T(8,128)(2,1)} %q_hbm.1, bf16[32,2,128,128]{3,2,1,0:T(8,128)(2,1)} %bitcast.2, s32[16,32]{1,0:T(8,128)} %sel_hbm.1, s32[16,32]{1,0:T(8,128)} %cnt_hbm.1, bf16[1024,4096]{1,0:T(8,128)(2,1)} %w_hbm.1), custom_call_target="tpu_custom_call" | custom-call | tf_op jit(solution)/shard_map/pallas_call | solution.py:416
  41.9 1.4 %copy.9 = bf16[16,1024]{1,0:T(8,128)(2,1)} copy(bf16[16,1024]{1,0:T(8,128)(2,1)} %get-tuple-element.8) | data formatting | bytes 65536
  43.3 1.2 %copy.10 = f32[32]{0:T(128)} copy(f32[32]{0:T(128)} %bitcast.3) | data formatting | bytes 256

commit v3 on v2

--- a/solution.py
+++ b/solution.py
@@ -16,11 +16,10 @@
 def offsets_in_order(side):
     far = list(range(2, side - 1))
     near = [1] + ([side - 1] if side > 2 else [])
-    row = near + far
-    order = [(0, 0)] + [(dx, 0) for dx in row]
-    for dz in far:
-        order += [(dx, dz) for dx in [0] + row]
-    order += [(dx, dz) for dx in row for dz in near]
+    order = [(0, 0)] + [(dx, 0) for dx in near + far] + [(0, dz) for dz in far]
+    order += [(dx, dz) for dx in near for dz in near]
+    order += [(dx, dz) for dx in near for dz in far]
+    order += [(dx, dz) for dx in far for dz in near + far]
     return order + [(0, dz) for dz in near]
 
 
@@ -130,6 +129,13 @@
             barrier, inc=1, device_id={"head": (y + j) % heads_n}, device_id_type=MESH
         )
 
+    pl.semaphore_wait(barrier, 2 * (side - 1) + heads_n)
+
+    first_sends = list(range(1, side)) + [i for i in range(n) if i and order[i][0] == 0]
+    for k in first_sends:
+        plane(k, 1).start()
+    fw(0, 1, True).start()
+
     devices = 2 * n
     loc[0].wait()
     sel = sel_v[...]
@@ -149,13 +155,9 @@
     tin[0] = town[cx]
     meta(0, 0).start()
 
-    pl.semaphore_wait(barrier, 2 * (side - 1) + heads_n)
-
-    for k in list(range(1, side)) + [i for i in range(n) if i and order[i][0] == 0]:
-        for s in range(2):
-            plane(k, s).start()
-    for s in range(2):
-        fw(0, s, True).start()
+    for k in first_sends:
+        plane(k, 0).start()
+    fw(0, 0, True).start()
 
     wcopies = [
         pltpu.make_async_copy(
@@ -239,83 +241,80 @@
         for c in to_owner(k):
             c.start()
 
+    def turn(start, stop):
+        @pl.loop(start, stop)
+        def _(b):
+            for i in range(4):
+                kt[b * 4 + i] = kv[b * 4 + i, 0].T
+
     loc[1].wait()
-
-    @pl.loop(0, blocks // 4)
-    def _(b):
-        for i in range(4):
-            kt[b * 4 + i] = kv[b * 4 + i, 0].T
-
+    turn(0, blocks // 4)
+
+    fw(0, 0).wait_recv()
+    meta(0, 1).start()
     hits[...] = jnp.zeros(hits.shape, f32)
     loc[2].wait()
     meta(0, 0).wait()
     scores(qin, 0, 0, p_in, own_ml)
 
-    for k in range(1, side):
-        for s in range(2):
+    for s in range(2):
+        for k in range(1, side):
             arrived(k, s).wait_recv()
             for i in range(n):
                 if order[i][0] == order[k][0] and order[i][1]:
                     plane(i, s).start()
             fw(k, s).start()
-        meta(k, 0).start()
-
-    for s in range(2):
-        fw(0, s).wait_recv()
-    meta(0, 1).start()
-    meta(0, 1).wait()
-    scores(qout, 1, 0, p_out, part_ml)
-    values(1, 0, load(p_out), emit_part)
-    for c in to_sibling(0):
-        c.start()
-    count(0)
-    fw(1, 0).wait_recv()
-    meta(1, 1).start()
-
-    @pl.loop(1, n)
+            if s == 0:
+                meta(k, 0).start()
+    @pl.loop(0, n - 1)
     def _(t):
-        ahead = t + side - 1
-
-        @pl.when(ahead < n)
+        @pl.when((t + 2 >= side) & (t + 2 < n))
         def _():
-            for s in range(2):
-                arrived(ahead, s).wait_recv()
-                fw(ahead, s).start()
-            meta(ahead, 0).start()
-
-        @pl.when(t + 1 < n)
+            arrived(t + 2, 0).wait_recv()
+            fw(t + 2, 0).start()
+            meta(t + 2, 0).start()
+
+        fw(t + 1, 0).wait_recv()
+        meta(t + 1, 1).start()
+
+        @pl.when(t + 1 >= side)
         def _():
-            fw(t + 1, 0).wait_recv()
-            meta(t + 1, 1).start()
-
-        @pl.when(t >= 2)
-        def _():
-            for c in to_sibling(t - 2):
-                c.wait_recv()
+            arrived(t + 1, 1).wait_recv()
+            fw(t + 1, 1).start()
 
         fw(t, 1).wait_recv()
-        meta(t, 0).wait()
         meta(t, 1).wait()
+        meta(t + 1, 0).wait()
 
         p = load(p_in)
         scores(qout, 1, t, p_out, part_ml)
-        values(0, t - 1, p, emit_own)
+        values(0, t, p, emit_own)
         p = load(p_out)
-        scores(qin, 0, t, p_in, own_ml)
+        scores(qin, 0, t + 1, p_in, own_ml)
         values(1, t, p, emit_part)
         count(t)
         for c in to_sibling(t):
             c.start()
 
+        @pl.when(t >= 1)
+        def _():
+            for c in to_sibling(t - 1):
+                c.wait_recv()
+            combine(t - 1)
+
         @pl.when(t >= 2)
         def _():
-            combine(t - 2)
-
-        @pl.when(t >= 3)
-        def _():
-            send_owner(t - 2)
-
-    values(0, n - 1, load(p_in), emit_own)
+            send_owner(t - 1)
+
+    fw(n - 1, 1).wait_recv()
+    meta(n - 1, 1).wait()
+    p = load(p_in)
+    scores(qout, 1, n - 1, p_out, part_ml)
+    values(0, n - 1, p, emit_own)
+    values(1, n - 1, load(p_out), emit_part)
+    count(n - 1)
+    for c in to_sibling(n - 1):
+        c.start()
     for k in (n - 2, n - 1):
         for c in to_sibling(k):
             c.wait_recv()
@@ -397,6 +396,11 @@
                 fw(k, s).wait_send()
             for c in to_owner(k):
                 c.wait_send()
+
+
+def hand_over(out_ref, heat_ref, out, heat):
+    out[...] = out_ref[...]
+    heat[...] = heat_ref[...]
 
 
 def per_device(side, heads_n, queries, cache_blocks, selected, counts, output_weight):
@@ -445,7 +449,12 @@
         ],
         compiler_params=pltpu.CompilerParams(collective_id=0, has_side_effects=True),
     )(queries, kv, selected, counts, output_weight)
-    return out, heat.reshape(blocks)
+    return pl.pallas_call(
+        hand_over,
+        out_shape=(jax.ShapeDtypeStruct(out.shape, bf), jax.ShapeDtypeStruct((blocks,), f32)),
+        in_specs=(vmem, vmem),
+        out_specs=(vmem, vmem),
+    )(out, heat.reshape(blocks))
 
 
 def solution(mesh):

time: 44.7 us -> 42 us (0.940)
  local copies, waits for them, and re-layouts: 2.55 us -> 0 us
    unnamed x2 -> x0, local copies, waits for them, and re-layouts: 2.55 us -> none
    pallas_call x1, Pallas kernels: 41.3 us -> 39.8 us  [per_device(): pl.pallas_call(functools.partial(kernel, side, heads_n, dim ** (-0.5), ma...]
    pallas_call x0 -> x1, Pallas kernels: none -> 1.38 us  [per_device(): pl.pallas_call(hand_over, out_shape=(jax.ShapeDtypeStruct(out.shape, bf),...]
where the time goes in v3:
time: 42 us; the launch traced here: 41.8 us
  Pallas kernels  41.1 us (98%)
  between operations  0.64 us (2%)
    pallas_call x1, Pallas kernels, per_device(): pl.pallas_call(functools.partial(kernel, side, heads_n, dim ** (-0.5), ma...  39.8 us
    pallas_call x1, Pallas kernels, per_device(): pl.pallas_call(hand_over, out_shape=(jax.ShapeDtypeStruct(out.shape, bf),...  1.38 us

profile of v3, /device:TPU:1, one launch (start us, length us, event | category | flops | bytes accessed | tf_op | source)
XLA Modules:
  0.0 41.8 jit_solution(2134958367752607132)
XLA Ops:
  0.6 39.8 %shard_map.68 = (bf16[16,1024]{1,0:T(8,128)(2,1)}, f32[1,32]{1,0:T(1,128)}) custom-call(bf16[16,8,128]{2,1,0:T(8,128)(2,1)} %q_hbm.1, bf16[32,2,128,128]{3,2,1,0:T(8,128)(2,1)} %bitcast.2, s32[16,32]{1,0:T(8,128)} %sel_hbm.1, s32[16,32]{1,0:T(8,128)} %cnt_hbm.1, bf16[1024,4096]{1,0:T(8,128)(2,1)} %w_hbm.1), custom_call_target="tpu_custom_call" | custom-call | tf_op jit(solution)/shard_map/pallas_call | solution.py:420
  40.4 1.4 %shard_map.69 = (bf16[16,1024]{1,0:T(8,128)(2,1)}, f32[32]{0:T(128)}) custom-call(bf16[16,1024]{1,0:T(8,128)(2,1)} %get-tuple-element.4.out_ref, f32[32]{0:T(128)} %bitcast.3), custom_call_target="tpu_custom_call" | custom-call | tf_op jit(solution)/shard_map/pallas_call | solution.py:452

commit v4 on v3

--- a/solution.py
+++ b/solution.py
@@ -116,9 +116,6 @@
         pltpu.make_async_copy(q_hbm, qin.at[0], lsem.at[2]),
         pltpu.make_async_copy(cnt_hbm, cnt, lsem.at[3]),
     ]
-    for c in loc:
-        c.start()
-
     barrier = pltpu.get_barrier_semaphore()
     pl.semaphore_signal(barrier, inc=1, device_id={"mem": sibling}, device_id_type=MESH)
     for d in range(1, side):
@@ -128,6 +125,9 @@
         pl.semaphore_signal(
             barrier, inc=1, device_id={"head": (y + j) % heads_n}, device_id_type=MESH
         )
+
+    for c in loc:
+        c.start()
 
     pl.semaphore_wait(barrier, 2 * (side - 1) + heads_n)
 
@@ -286,6 +286,12 @@
         meta(t, 1).wait()
         meta(t + 1, 0).wait()
 
+        @pl.when(t >= 2)
+        def _():
+            for c in to_sibling(t - 2):
+                c.wait_recv()
+
+        combine(jnp.where(t >= 2, t - 2, n))
         p = load(p_in)
         scores(qout, 1, t, p_out, part_ml)
         values(0, t, p, emit_own)
@@ -296,18 +302,15 @@
         for c in to_sibling(t):
             c.start()
 
-        @pl.when(t >= 1)
+        @pl.when(t >= 3)
         def _():
-            for c in to_sibling(t - 1):
-                c.wait_recv()
-            combine(t - 1)
-
-        @pl.when(t >= 2)
-        def _():
-            send_owner(t - 1)
+            send_owner(t - 2)
 
     fw(n - 1, 1).wait_recv()
     meta(n - 1, 1).wait()
+    for c in to_sibling(n - 3):
+        c.wait_recv()
+    combine(n - 3)
     p = load(p_in)
     scores(qout, 1, n - 1, p_out, part_ml)
     values(0, n - 1, p, emit_own)
@@ -315,6 +318,7 @@
     count(n - 1)
     for c in to_sibling(n - 1):
         c.start()
+    send_owner(n - 3)
     for k in (n - 2, n - 1):
         for c in to_sibling(k):
             c.wait_recv()
@@ -415,7 +419,8 @@
     vmem = pl.BlockSpec(memory_space=pltpu.VMEM)
     dma = pltpu.SemaphoreType.DMA
     rows = pltpu.VMEM((n, reqs, heads, dim), bf)
-    small = pltpu.VMEM((n, heads, 128), f32)
+    small = pltpu.VMEM((n + 1, heads, 128), f32)
+    spare = pltpu.VMEM((n + 1, reqs, heads, dim), bf)
     tiles = pltpu.VMEM((n, 2 * side, 128), i32)
     out, heat = pl.pallas_call(
         functools.partial(kernel, side, heads_n, dim ** -0.5, max(2, n // 4)),
@@ -437,8 +442,8 @@
             pltpu.SMEM((2, n, 1, 128), i32),
             pltpu.VMEM((reqs // 2, 2 * heads, 2 * tok), bf),
             pltpu.VMEM((reqs // 2, 2 * heads, 2 * tok), bf),
-            pltpu.VMEM((n, reqs, heads, dim), f32),
-            small, rows, small, rows, small, rows, small, rows, small,
+            pltpu.VMEM((n + 1, reqs, heads, dim), f32),
+            small, rows, small, spare, small, spare, small, rows, small,
             pltpu.VMEM((reqs, heads, dim), f32),
             pltpu.VMEM((heads_n, reqs, cols), bf),
             pltpu.VMEM((heads_n, reqs, cols), bf),

time: 42 us -> 42.1 us (level)
  no operation moved by 1% of the time
where the time goes in v4:
time: 42.1 us; the launch traced here: 41.9 us
  Pallas kernels  41.3 us (98%)
  between operations  0.64 us (2%)
    pallas_call x1, Pallas kernels, per_device(): pl.pallas_call(functools.partial(kernel, side, heads_n, dim ** (-0.5), ma...  39.9 us
    pallas_call x1, Pallas kernels, per_device(): pl.pallas_call(hand_over, out_shape=(jax.ShapeDtypeStruct(out.shape, bf),...  1.38 us

profile of v4, /device:TPU:1, one launch (start us, length us, event | category | flops | bytes accessed | tf_op | source)
XLA Modules:
  0.0 41.9 jit_solution(7382201719267229329)
XLA Ops:
  0.6 39.9 %shard_map.68 = (bf16[16,1024]{1,0:T(8,128)(2,1)}, f32[1,32]{1,0:T(1,128)}) custom-call(bf16[16,8,128]{2,1,0:T(8,128)(2,1)} %q_hbm.1, bf16[32,2,128,128]{3,2,1,0:T(8,128)(2,1)} %bitcast.2, s32[16,32]{1,0:T(8,128)} %sel_hbm.1, s32[16,32]{1,0:T(8,128)} %cnt_hbm.1, bf16[1024,4096]{1,0:T(8,128)(2,1)} %w_hbm.1), custom_call_target="tpu_custom_call" | custom-call | tf_op jit(solution)/shard_map/pallas_call | solution.py:425
  40.6 1.4 %shard_map.69 = (bf16[16,1024]{1,0:T(8,128)(2,1)}, f32[32]{0:T(128)}) custom-call(bf16[16,1024]{1,0:T(8,128)(2,1)} %get-tuple-element.4.out_ref, f32[32]{0:T(128)} %bitcast.3), custom_call_target="tpu_custom_call" | custom-call | tf_op jit(solution)/shard_map/pallas_call | solution.py:457

commit v5 on v4

--- a/solution.py
+++ b/solution.py
@@ -110,12 +110,23 @@
             remote(comb_ml.at[k], ret_ml.at[k], rt_s.at[1, k], rt_r.at[1, k], mem=peer),
         )
 
+    def straight():
+        dx, dz = order[n - 1]
+        peer = chip_at(-dx, -dz) + 1 - 2 * core
+        return (
+            remote(part.at[n - 1], ret.at[n], sb_s.at[0, n - 1], sb_r.at[0, n - 1], mem=peer),
+            remote(part_ml.at[n - 1], ret_ml.at[n], sb_s.at[1, n - 1], sb_r.at[1, n - 1], mem=peer),
+        )
+
     loc = [
         pltpu.make_async_copy(sel_hbm, sel_v, lsem.at[0]),
         pltpu.make_async_copy(kv_hbm, kv, lsem.at[1]),
         pltpu.make_async_copy(q_hbm, qin.at[0], lsem.at[2]),
         pltpu.make_async_copy(cnt_hbm, cnt, lsem.at[3]),
     ]
+    for c in loc:
+        c.start()
+
     barrier = pltpu.get_barrier_semaphore()
     pl.semaphore_signal(barrier, inc=1, device_id={"mem": sibling}, device_id_type=MESH)
     for d in range(1, side):
@@ -125,9 +136,6 @@
         pl.semaphore_signal(
             barrier, inc=1, device_id={"head": (y + j) % heads_n}, device_id_type=MESH
         )
-
-    for c in loc:
-        c.start()
 
     pl.semaphore_wait(barrier, 2 * (side - 1) + heads_n)
 
@@ -220,6 +228,9 @@
     def emit_part(k, r, o):
         part[k, r] = o.astype(bf)
 
+    def emit_last(k, r, o):
+        comb[k, r] = o.astype(bf)
+
     def load(p_ref):
         return [p_ref[i] for i in range(reqs // 2)]
 
@@ -313,17 +324,18 @@
     combine(n - 3)
     p = load(p_in)
     scores(qout, 1, n - 1, p_out, part_ml)
-    values(0, n - 1, p, emit_own)
+    values(0, n - 1, p, emit_last)
     values(1, n - 1, load(p_out), emit_part)
+    comb_ml[n - 1] = own_ml[n - 1]
     count(n - 1)
-    for c in to_sibling(n - 1):
+    for c in straight():
         c.start()
+    send_owner(n - 1)
     send_owner(n - 3)
-    for k in (n - 2, n - 1):
-        for c in to_sibling(k):
-            c.wait_recv()
-        combine(k)
-        send_owner(k)
+    for c in to_sibling(n - 2):
+        c.wait_recv()
+    combine(n - 2)
+    send_owner(n - 2)
 
     loc[3].wait()
     counts = cnt[...].astype(f32)
@@ -338,9 +350,13 @@
     ret_ml[0] = comb_ml[0]
 
     def merged(start, stop):
-        @pl.loop(max(start, 1), stop)
+        @pl.loop(max(start, 1), min(stop, n))
         def _(k):
             for c in to_owner(k):
+                c.wait_recv()
+
+        if stop > n:
+            for c in straight():
                 c.wait_recv()
 
         top = ret_ml[start]
@@ -359,7 +375,7 @@
         return top, den, acc
 
     top_a, den_a, acc_a = merged(0, n - later)
-    top_b, den_b, acc_b = merged(n - later, n)
+    top_b, den_b, acc_b = merged(n - later, n + 1)
     top = jnp.maximum(top_a, top_b)
     fa, fb = jnp.exp2((top_a - top) * c2), jnp.exp2((top_b - top) * c2)
     inv = 1.0 / (fa * den_a + fb * den_b)
@@ -375,7 +391,7 @@
     def y_copy(j):
         return remote(ysend.at[j], yrecv.at[j], y_s.at[j], y_r.at[j], head=(y + j) % heads_n)
 
-    for j in range(1, heads_n):
+    for j in sorted(range(1, heads_n), key=lambda j: -min(j, heads_n - j)):
         ysend[j] = jnp.dot(lhs, w[j], preferred_element_type=f32).astype(bf)
         y_copy(j).start()
     total = jnp.dot(lhs, w[0], preferred_element_type=f32).astype(bf).astype(f32)
@@ -389,17 +405,17 @@
         for k in range(1, n):
             plane(k, s).wait_send()
 
-    @pl.loop(0, n)
+    for c in straight():
+        c.wait_send()
+
+    @pl.loop(1, n)
     def _(k):
-        for c in to_sibling(k):
+        for c in to_sibling(k - 1):
             c.wait_send()
-
-        @pl.when(k > 0)
-        def _():
-            for s in range(2):
-                fw(k, s).wait_send()
-            for c in to_owner(k):
-                c.wait_send()
+        for s in range(2):
+            fw(k, s).wait_send()
+        for c in to_owner(k):
+            c.wait_send()
 
 
 def hand_over(out_ref, heat_ref, out, heat):
@@ -423,7 +439,7 @@
     spare = pltpu.VMEM((n + 1, reqs, heads, dim), bf)
     tiles = pltpu.VMEM((n, 2 * side, 128), i32)
     out, heat = pl.pallas_call(
-        functools.partial(kernel, side, heads_n, dim ** -0.5, max(2, n // 4)),
+        functools.partial(kernel, side, heads_n, dim ** -0.5, max(1, n // 5)),
         out_shape=(
             jax.ShapeDtypeStruct((reqs, cols), bf),
             jax.ShapeDtypeStruct((1, blocks), f32),
@@ -443,7 +459,7 @@
             pltpu.VMEM((reqs // 2, 2 * heads, 2 * tok), bf),
             pltpu.VMEM((reqs // 2, 2 * heads, 2 * tok), bf),
             pltpu.VMEM((n + 1, reqs, heads, dim), f32),
-            small, rows, small, spare, small, spare, small, rows, small,
+            small, rows, small, spare, small, spare, small, spare, small,
             pltpu.VMEM((reqs, heads, dim), f32),
             pltpu.VMEM((heads_n, reqs, cols), bf),
             pltpu.VMEM((heads_n, reqs, cols), bf),

time: 42.1 us -> 42.1 us (level)
  no operation moved by 1% of the time
where the time goes in v5:
time: 42.1 us; the launch traced here: 41.9 us
  Pallas kernels  41.2 us (98%)
  between operations  0.64 us (2%)
    pallas_call x1, Pallas kernels, per_device(): pl.pallas_call(functools.partial(kernel, side, heads_n, dim ** (-0.5), ma...  39.9 us
    pallas_call x1, Pallas kernels, per_device(): pl.pallas_call(hand_over, out_shape=(jax.ShapeDtypeStruct(out.shape, bf),...  1.38 us

profile of v5, /device:TPU:1, one launch (start us, length us, event | category | flops | bytes accessed | tf_op | source)
XLA Modules:
  0.0 41.9 jit_solution(13756294049949834612)
XLA Ops:
  0.6 39.9 %shard_map.68 = (bf16[16,1024]{1,0:T(8,128)(2,1)}, f32[1,32]{1,0:T(1,128)}) custom-call(bf16[16,8,128]{2,1,0:T(8,128)(2,1)} %q_hbm.1, bf16[32,2,128,128]{3,2,1,0:T(8,128)(2,1)} %bitcast.2, s32[16,32]{1,0:T(8,128)} %sel_hbm.1, s32[16,32]{1,0:T(8,128)} %cnt_hbm.1, bf16[1024,4096]{1,0:T(8,128)(2,1)} %w_hbm.1), custom_call_target="tpu_custom_call" | custom-call | tf_op jit(solution)/shard_map/pallas_call | solution.py:441
  40.5 1.4 %shard_map.69 = (bf16[16,1024]{1,0:T(8,128)(2,1)}, f32[32]{0:T(128)}) custom-call(bf16[16,1024]{1,0:T(8,128)(2,1)} %get-tuple-element.4.out_ref, f32[32]{0:T(128)} %bitcast.3), custom_call_target="tpu_custom_call" | custom-call | tf_op jit(solution)/shard_map/pallas_call | solution.py:473
